TPU v7x, 32 devices: a whole 2x2x4 slice. The times are simulated.
32 devices in a mesh: batch: 8 (over z, y), tensor: 4 (over x, core).
Axes of the slice: x: 2, y: 2, z: 4, core: 2. Of those that a mesh axis runs over, the one named last changes fastest.
Arguments:
- tokens: bfloat16 [12288, 768], P('batch'), may hold values from -6 to 6
- lengths: int32 [8], P('batch'), may hold values from 1024 to 1536, as said below
- w_query: bfloat16 [768, 768], P('batch', 'tensor'), may hold values from -0.4375 to 0.4375
- w_key: bfloat16 [768, 768], P('batch', 'tensor'), may hold values from -0.21875 to 0.21875
- w_value: bfloat16 [768, 768], P('batch', 'tensor'), may hold values from -0.21875 to 0.21875
- w_out: bfloat16 [768, 768], P('tensor', 'batch'), may hold values from -0.875 to 0.875
- w_up: bfloat16 [768, 3072], P('batch', 'tensor'), may hold values from -0.21875 to 0.21875
- w_down: bfloat16 [3072, 768], P('tensor', 'batch'), may hold values from -0.109375 to 0.109375
- norm_gain: bfloat16 [2, 768], P(None, 'batch'), may hold values from 0.099609375 to 1.8984375
- norm_shift: bfloat16 [2, 768], P(None, 'batch'), may hold values from -3 to 3
- out_grad: bfloat16 [12288, 768], P('batch'), may hold values from -6 to 6
Outputs:
- layer_out: bfloat16 [12288, 768], P('batch')
- grad_input: bfloat16 [12288, 768], P('batch')
- grad_query: float32 [768, 768], P('batch', 'tensor')
- grad_key: float32 [768, 768], P('batch', 'tensor')
- grad_value: float32 [768, 768], P('batch', 'tensor')
- grad_out: float32 [768, 768], P('tensor', 'batch')
- grad_up: float32 [768, 3072], P('batch', 'tensor')
- grad_down: float32 [3072, 768], P('tensor', 'batch')
- grad_gain: float32 [2, 768], P(None, 'batch')
- grad_shift: float32 [2, 768], P(None, 'batch')
Inputs may be any that keep to these rules, and one draw needn't show every extreme that they name: `lengths`: each sequence's valid tokens; some sequence fills all 1536 slots.
All inputs are finite; a program needn't handle non-finite values.
Results may differ from a plain program's by a relative error of at most 0.017.
Values may be sent and summed in bfloat16 or wider, within the bound.
No kernel may reach another device: no remote copies, remote signals or barrier semaphores. Data moves between devices by JAX's collectives and lax.ppermute only.
A program may use at most 192 MiB of HBM per device.

v0:
```python
import jax
import jax.numpy as jnp
from jax import lax
from jax.sharding import PartitionSpec as P

HD = 64
epsilon = 1e-05


def cut_along(value, dim, length):
    shape = value.shape
    parts = value.reshape(*shape[:dim], length, shape[dim] // length, *shape[dim + 1 :])
    return jnp.moveaxis(parts, dim, 0)


def summed_on_arrival(value, axis, dim):
    length = lax.axis_size(axis)
    parts = lax.all_to_all(cut_along(value, dim, length), axis, 0, 0, tiled=True)
    return jnp.sum(parts.astype(jnp.float32), axis=0)


def normalize_keep(values, gain_row, shift_row):
    middle = jnp.mean(values, axis=-1, keepdims=True)
    centred = values - middle
    spread = jnp.mean(centred * centred, axis=-1, keepdims=True)
    inverse = lax.rsqrt(spread + epsilon)
    scaled = centred * inverse
    return (scaled * gain_row + shift_row, scaled, inverse)


def normalize_back(grad_normed, scaled, inverse, gain_row):
    grad_scaled = grad_normed * gain_row
    mean_grad = jnp.mean(grad_scaled, axis=-1, keepdims=True)
    mean_cross = jnp.mean(grad_scaled * scaled, axis=-1, keepdims=True)
    grad_values = inverse * (grad_scaled - mean_grad - scaled * mean_cross)
    return (grad_values, jnp.sum(grad_normed * scaled, axis=0), jnp.sum(grad_normed, axis=0))


def multiply(left_mat, right_mat):
    return jnp.dot(left_mat, right_mat, preferred_element_type=jnp.float32)


def inner_rows(left_mat, right_mat):
    return lax.dot_general(
        left_mat, right_mat, (((0,), (0,)), ((), ())), preferred_element_type=jnp.float32
    )


def outer_cols(left_mat, right_mat):
    return lax.dot_general(
        left_mat, right_mat, (((1,), (1,)), ((), ())), preferred_element_type=jnp.float32
    )


def gelu_tanh(values):
    return jax.nn.gelu(values, approximate=True)


def score_block(queries_blk, keys_part, row_pos, key_pos, length, scaling):
    raw_scores = jnp.einsum(
        "qhd,khd->hqk", queries_blk, keys_part, preferred_element_type=jnp.float32
    )
    scores = raw_scores * scaling
    allowed = (key_pos[None, :] <= row_pos[:, None]) & (key_pos[None, :] < length)
    magnitude = jnp.where(allowed[None], jnp.abs(scores), -1e30)
    return (scores, magnitude)


def attend_forward(queries, key_rows, value_rows, length, block_rows, scaling):
    seq_rows = queries.shape[0]
    position = jnp.arange(seq_rows, dtype=jnp.int32)
    outputs = []
    log_sums = []
    for number in range(seq_rows // block_rows):
        begin_row = number * block_rows
        end_row = begin_row + block_rows
        scores, magnitude = score_block(
            queries[begin_row:end_row],
            key_rows[:end_row],
            position[begin_row:end_row],
            position[:end_row],
            length,
            scaling,
        )
        row_max = jnp.max(magnitude, axis=-1, keepdims=True)
        exponent = jnp.exp(magnitude - row_max)
        row_sum = jnp.sum(exponent, axis=-1, keepdims=True)
        weights = (jnp.sign(scores) * (exponent / row_sum)).astype(jnp.bfloat16)
        outputs.append(
            jnp.einsum(
                "hqk,khd->qhd", weights, value_rows[:end_row], preferred_element_type=jnp.float32
            )
        )
        log_sums.append(row_max + jnp.log(row_sum))
    return (jnp.concatenate(outputs, axis=0), jnp.concatenate(log_sums, axis=1))


def attend_back(queries, key_rows, value_rows, grad_mixed, log_sums, length, block_rows, scaling):
    seq_rows = queries.shape[0]
    position = jnp.arange(seq_rows, dtype=jnp.int32)
    grad_queries = []
    grad_keys = jnp.zeros(key_rows.shape, jnp.float32)
    grad_values = jnp.zeros(value_rows.shape, jnp.float32)
    for number in range(seq_rows // block_rows):
        begin_row = number * block_rows
        end_row = begin_row + block_rows
        scores, magnitude = score_block(
            queries[begin_row:end_row],
            key_rows[:end_row],
            position[begin_row:end_row],
            position[:end_row],
            length,
            scaling,
        )
        probability = jnp.exp(magnitude - log_sums[:, begin_row:end_row])
        signs = jnp.sign(scores)
        weights = signs * probability
        grad_blk = grad_mixed[begin_row:end_row]
        grad_weights = jnp.einsum(
            "qhd,khd->hqk", grad_blk, value_rows[:end_row], preferred_element_type=jnp.float32
        )
        delta_row = jnp.sum(weights * grad_weights, axis=-1, keepdims=True)
        grad_raw = (signs * probability * (signs * grad_weights - delta_row) * scaling).astype(
            jnp.bfloat16
        )
        grad_queries.append(
            jnp.einsum(
                "hqk,khd->qhd", grad_raw, key_rows[:end_row], preferred_element_type=jnp.float32
            )
        )
        grad_keys = grad_keys.at[:end_row].add(
            jnp.einsum(
                "hqk,qhd->khd",
                grad_raw,
                queries[begin_row:end_row],
                preferred_element_type=jnp.float32,
            )
        )
        grad_values = grad_values.at[:end_row].add(
            jnp.einsum(
                "hqk,qhd->khd",
                weights.astype(jnp.bfloat16),
                grad_blk,
                preferred_element_type=jnp.float32,
            )
        )
    return (jnp.concatenate(grad_queries, axis=0), grad_keys, grad_values)


def per_device(
    tokens, lengths, w_query, w_key, w_value, w_out, w_up, w_down, norm_gain, norm_shift, out_grad
):
    seq_rows = tokens.shape[0]
    seq_count = lengths.shape[0]
    seq_len = seq_rows // seq_count
    position = jnp.arange(seq_rows, dtype=jnp.int32)
    slot_length = jnp.repeat(lengths, seq_len)
    is_valid = (position % seq_len < slot_length).astype(jnp.float32)[:, None]
    block_rows = min(512, seq_len)
    scaling = float(HD) ** (-0.5)
    gathered = (
        lax.all_gather(w_query, "batch", axis=0, tiled=True),
        lax.all_gather(w_key, "batch", axis=0, tiled=True),
        lax.all_gather(w_value, "batch", axis=0, tiled=True),
        lax.all_gather(w_out, "batch", axis=1, tiled=True),
        lax.all_gather(w_up, "batch", axis=0, tiled=True),
        lax.all_gather(w_down, "batch", axis=1, tiled=True),
        lax.all_gather(norm_gain, "batch", axis=1, tiled=True),
        lax.all_gather(norm_shift, "batch", axis=1, tiled=True),
    )
    full_query, full_key, full_value, full_out, full_up, full_down, gain_full, shift_full = gathered
    gain_rows = gain_full.astype(jnp.float32)
    shift_rows = shift_full.astype(jnp.float32)
    head_count = full_query.shape[1] // HD

    def per_sequence(values):
        return values.reshape(seq_count, seq_len, head_count, HD)

    inputs = tokens.astype(jnp.float32)
    normed, scaled_one, inverse_one = normalize_keep(inputs, gain_rows[0], shift_rows[0])
    normed_low = normed.astype(jnp.bfloat16)
    queries = (
        multiply(normed_low, full_query).astype(jnp.bfloat16).reshape(seq_rows, head_count, HD)
    )
    key_rows = multiply(normed_low, full_key).astype(jnp.bfloat16).reshape(seq_rows, head_count, HD)
    value_rows = (
        multiply(normed_low, full_value).astype(jnp.bfloat16).reshape(seq_rows, head_count, HD)
    )

    def forward_one(items):
        return attend_forward(items[0], items[1], items[2], items[3], block_rows, scaling)

    mixed_heads, log_sums = lax.map(
        forward_one,
        (per_sequence(queries), per_sequence(key_rows), per_sequence(value_rows), lengths),
    )
    mixed_low = mixed_heads.reshape(seq_rows, head_count * HD).astype(jnp.bfloat16)
    attn_partial = multiply(mixed_low, full_out)
    hidden = inputs + lax.psum(attn_partial, "tensor")
    normed_two, scaled_two, inverse_two = normalize_keep(hidden, gain_rows[1], shift_rows[1])
    normed_two_low = normed_two.astype(jnp.bfloat16)
    up_proj = multiply(normed_two_low, full_up)
    active_full, gelu_pull = jax.vjp(gelu_tanh, up_proj)
    active = active_full.astype(jnp.bfloat16)
    down_partial = multiply(active, full_down)
    branch = lax.psum(down_partial.astype(jnp.bfloat16), "tensor").astype(jnp.float32)
    out_rows = ((hidden + branch) * is_valid).astype(jnp.bfloat16)
    grad_rows = out_grad * is_valid.astype(jnp.bfloat16)
    grad_down = inner_rows(active, grad_rows)
    grad_active = outer_cols(grad_rows, full_down)
    grad_upper = gelu_pull(grad_active)[0].astype(jnp.bfloat16)
    grad_up = inner_rows(normed_two_low, grad_upper)
    mid_partial = outer_cols(grad_upper, full_up)
    grad_normed_two = lax.psum(mid_partial, "tensor")
    grad_from_two, gain_two, shift_two = normalize_back(
        grad_normed_two, scaled_two, inverse_two, gain_rows[1]
    )
    grad_hidden = grad_rows.astype(jnp.float32) + grad_from_two
    grad_attn = grad_hidden.astype(jnp.bfloat16)
    grad_out = inner_rows(mixed_low, grad_attn)
    grad_mixed = (
        outer_cols(grad_attn, full_out).astype(jnp.bfloat16).reshape(seq_rows, head_count, HD)
    )

    def backward_one(items):
        return attend_back(
            items[0], items[1], items[2], items[3], items[4], items[5], block_rows, scaling
        )

    grad_queries, grad_keys, grad_values = lax.map(
        backward_one,
        (
            per_sequence(queries),
            per_sequence(key_rows),
            per_sequence(value_rows),
            per_sequence(grad_mixed),
            log_sums,
            lengths,
        ),
    )
    queries_low = grad_queries.astype(jnp.bfloat16).reshape(seq_rows, head_count * HD)
    keys_low = grad_keys.astype(jnp.bfloat16).reshape(seq_rows, head_count * HD)
    values_low = grad_values.astype(jnp.bfloat16).reshape(seq_rows, head_count * HD)
    grad_query = inner_rows(normed_low, queries_low)
    grad_key = inner_rows(normed_low, keys_low)
    grad_value = inner_rows(normed_low, values_low)
    partial_in = (
        outer_cols(queries_low, full_query)
        + outer_cols(keys_low, full_key)
        + outer_cols(values_low, full_value)
    )
    grad_normed = lax.psum(partial_in.astype(jnp.bfloat16), "tensor").astype(jnp.float32)
    grad_from_one, gain_one, shift_one = normalize_back(
        grad_normed, scaled_one, inverse_one, gain_rows[0]
    )
    grad_input = (grad_hidden + grad_from_one).astype(jnp.bfloat16)
    gain_pair = jnp.stack([gain_one, gain_two])
    shift_pair = jnp.stack([shift_one, shift_two])
    everything = (
        summed_on_arrival(grad_query.astype(jnp.bfloat16), "batch", 0),
        summed_on_arrival(grad_key.astype(jnp.bfloat16), "batch", 0),
        summed_on_arrival(grad_value.astype(jnp.bfloat16), "batch", 0),
        summed_on_arrival(grad_out.astype(jnp.bfloat16), "batch", 1),
        summed_on_arrival(grad_up.astype(jnp.bfloat16), "batch", 0),
        summed_on_arrival(grad_down.astype(jnp.bfloat16), "batch", 1),
        summed_on_arrival(gain_pair.astype(jnp.bfloat16), "batch", 1),
        summed_on_arrival(shift_pair.astype(jnp.bfloat16), "batch", 1),
    )
    (
        shard_query,
        shard_key,
        shard_value,
        shard_out,
        shard_up,
        shard_down,
        shard_gain,
        shard_shift,
    ) = everything
    return (
        out_rows,
        grad_input,
        shard_query,
        shard_key,
        shard_value,
        shard_out,
        shard_up,
        shard_down,
        shard_gain,
        shard_shift,
    )


def solution(mesh):
    in_specs = (
        P("batch", None),
        P("batch"),
        P("batch", "tensor"),
        P("batch", "tensor"),
        P("batch", "tensor"),
        P("tensor", "batch"),
        P("batch", "tensor"),
        P("tensor", "batch"),
        P(None, "batch"),
        P(None, "batch"),
        P("batch", None),
    )
    out_specs = (
        P("batch", None),
        P("batch", None),
        P("batch", "tensor"),
        P("batch", "tensor"),
        P("batch", "tensor"),
        P("tensor", "batch"),
        P("batch", "tensor"),
        P("tensor", "batch"),
        P(None, "batch"),
        P(None, "batch"),
    )
    return jax.shard_map(
        per_device, mesh=mesh, in_specs=in_specs, out_specs=out_specs, check_vma=False
    )
```

profile of v0, /device:TPU:0, one launch (start us, length us, event | category | flops | bytes accessed | tf_op | source)
XLA Modules:
  0.0 746.9 jit_solution(5650384383720290563)
XLA Ops:
  9.3 22.3 %all-gather = bf16[8,96,2]{1,2,0:T(2,128)(2,1)S(1)} all-gather(bf16[1,96,2]{1,2,0:T(2,128)(2,1)} %bitcast.189), channel_id=1, replica_groups=mesh['batch'=8,'tensor'=4] {'batch'}, dimensions={0}, use_global_device_ids=true | all-gather | bytes 3456 | tf_op jit(solution)/shard_map/all_gather | solution.py:168
  32.3 16.4 %all-gather.1 = bf16[8,96,2]{1,2,0:T(2,128)(2,1)S(1)} all-gather(bf16[1,96,2]{1,2,0:T(2,128)(2,1)} %bitcast.190), channel_id=1, replica_groups=mesh['batch'=8,'tensor'=4] {'batch'}, dimensions={0}, use_global_device_ids=true | all-gather | bytes 3456 | tf_op jit(solution)/shard_map/all_gather | solution.py:169
  54.0 31.0 %all_gather.28 = bf16[768,192]{1,0:T(8,128)(2,1)S(1)} all-gather(bf16[96,192]{1,0:T(8,128)(2,1)S(1)} %copy-done.50), channel_id=1, replica_groups=mesh['batch'=8,'tensor'=4] {'batch'}, dimensions={0}, use_global_device_ids=true | all-gather | bytes 331776 | tf_op jit(solution)/shard_map/all_gather | solution.py:163
  88.7 31.2 %all_gather.26 = bf16[768,192]{1,0:T(8,128)(2,1)S(1)} all-gather(bf16[96,192]{1,0:T(8,128)(2,1)S(1)} %copy-done.51), channel_id=1, replica_groups=mesh['batch'=8,'tensor'=4] {'batch'}, dimensions={0}, use_global_device_ids=true | all-gather | bytes 331776 | tf_op jit(solution)/shard_map/all_gather | solution.py:164
  125.1 31.3 %all_gather.29 = bf16[192,768]{0,1:T(8,128)(2,1)S(1)} all-gather(bf16[192,96]{0,1:T(8,128)(2,1)} %copy.70), channel_id=1, replica_groups=mesh['batch'=8,'tensor'=4] {'batch'}, dimensions={1}, use_global_device_ids=true | all-gather | bytes 331776 | tf_op jit(solution)/shard_map/all_gather | solution.py:165
  156.4 31.2 %all_gather.27 = bf16[768,192]{1,0:T(8,128)(2,1)S(1)} all-gather(bf16[96,192]{1,0:T(8,128)(2,1)} %param.29), channel_id=1, replica_groups=mesh['batch'=8,'tensor'=4] {'batch'}, dimensions={0}, use_global_device_ids=true | all-gather | bytes 331776 | tf_op jit(solution)/shard_map/all_gather | solution.py:162
  210.0 6.4 fusion.150
  222.0 90.3 %all-reduce.7.cloned.1.call-done = f32[1536,768]{1,0:T(8,128)} async-done(((f32[1536,768]{1,0:T(8,128)}), f32[1536,768]{1,0:T(8,128)}) %all-reduce.7.cloned.1.call-update) | async-done | bytes 4718608 | tf_op jit(solution)/shard_map/psum | solution.py:199
  319.5 6.2 fusion.203
  325.7 7.0 fusion.31
  341.1 6.8 fusion.107
  347.9 5.9 all-to-all-start.5
  353.8 5.6 convolution_convert_fusion.5
  359.4 6.8 convolution_convert_fusion
  366.1 66.6 %all-reduce.9.cloned.1.call-done = f32[1536,768]{1,0:T(8,128)} async-done(((f32[1536,768]{1,0:T(8,128)}), f32[1536,768]{1,0:T(8,128)}) %all-reduce.9.cloned.1.call-update) | async-done | bytes 4718608 | tf_op jit(solution)/shard_map/psum | solution.py:214
  432.7 5.6 multiply_reduce_fusion.2
  450.4 9.7 %fusion.128 = f32[512,3,64]{0,2,1:T(8,128)} fusion(bf16[512,3,64]{0,2,1:T(8,128)(2,1)} %bitcast.178, f32[3,512,512]{1,2,0:T(8,128)} %fusion.205, f32[3,512,512]{1,2,0:T(8,128)} %copy-done.18, f32[3,512]{1,0:T(4,128)S(1)} %copy-done.61, pred[512,512]{0,1:T(8,128)(4,1)} %copy-done.28), kind=kOutput, calls=%fused_computation.130 | convolution fusion | flops 114821120 | bytes 7149568 | tf_op jit(solution)/shard_map/while/body/eval_jaxpr/hqk,qhd->khd/dot_general | solution.py:132
  465.0 5.1 fusion.207
  470.0 20.1 %fusion.145 = bf16[3,64,512]{2,1,0:T(8,128)(2,1)} fusion(bf16[1024,3,64]{0,2,1:T(8,128)(2,1)} %bitcast.171, f32[3,512,1024]{2,1,0:T(8,128)} %fusion.206, f32[3,512,1024]{2,1,0:T(8,128)} %copy-done.7, f32[3,512]{1,0:T(4,128)} %log_add_fusion.1, pred[512,1024]{1,0:T(8,128)(4,1)} %copy-done.23), kind=kOutput, calls=%fused_computation.139 | convolution fusion | flops 229739008 | bytes 13703168 | tf_op jit(solution)/shard_map/while/body/eval_jaxpr/hqk,khd->qhd/dot_general | solution.py:127
  493.5 9.8 %fusion.141 = bf16[3,64,512]{2,1,0:T(8,128)(2,1)} fusion(bf16[512,3,64]{0,2,1:T(8,128)(2,1)} %bitcast.179, f32[3,512,512]{1,2,0:T(8,128)} %fusion.205, f32[3,512,512]{1,2,0:T(8,128)} %copy-done.18, f32[3,512]{1,0:T(4,128)S(1)} %copy-done.61, pred[512,512]{0,1:T(8,128)(4,1)} %copy-done.28), kind=kOutput, calls=%fused_computation.137 | convolution fusion | flops 114919424 | bytes 6952960 | tf_op jit(solution)/shard_map/while/body/eval_jaxpr/hqk,khd->qhd/dot_general | solution.py:127
  503.3 26.8 %fusion.138 = bf16[3,64,512]{2,1,0:T(8,128)(2,1)} fusion(bf16[1536,3,64]{0,2,1:T(8,128)(2,1)S(1)} %bitcast.154, f32[3,512,1536]{2,1,0:T(8,128)} %fusion.207, f32[3,512,1536]{2,1,0:T(8,128)} %copy-done.6, f32[3,512]{1,0:T(4,128)S(1)} %copy-done.62, pred[512,1536]{1,0:T(8,128)(4,1)} %copy-done.16), kind=kOutput, calls=%fused_computation.136 | convolution fusion | flops 344558592 | bytes 20453376 | tf_op jit(solution)/shard_map/while/body/eval_jaxpr/hqk,khd->qhd/dot_general | solution.py:127
  530.0 20.4 %fusion.119 = f32[1536,3,64]{0,2,1:T(8,128)} fusion(f32[1536,3,64]{0,2,1:T(8,128)} %scatter-add.14, bf16[512,3,64]{0,2,1:T(8,128)(2,1)} %bitcast.176, f32[3,512,1024]{2,1,0:T(8,128)} %fusion.206, f32[3,512,1024]{2,1,0:T(8,128)} %copy-done.7, f32[3,512]{1,0:T(4,128)S(1)} %copy-done.63, pred[512,1024]{1,0:T(8,128)(4,1)} %copy-done.23), kind=kOutput, calls=%fused_computation.123 | convolution fusion | flops 229837312 | bytes 28000256 | tf_op jit(solution)/shard_map/while/body/eval_jaxpr/hqk,qhd->khd/dot_general | solution.py:132
  550.5 27.8 %fusion.76 = bf16[1536,3,64]{0,2,1:T(8,128)(2,1)} fusion(f32[1536,3,64]{0,2,1:T(8,128)} %fusion.119, bf16[512,3,64]{0,2,1:T(8,128)(2,1)S(1)} %bitcast.174, f32[3,512,1536]{2,1,0:T(8,128)} %fusion.207, f32[3,512,1536]{2,1,0:T(8,128)} %copy-done.6, f32[3,512]{1,0:T(4,128)S(1)} %copy-done.62, pred[512,1536]{1,0:T(8,128)(4,1)} %copy-done.16), kind=kOutput, calls=%fused_computation.94 | convolution fusion | flops 345050112 | bytes 21633024 | tf_op jit(solution)/shard_map/while/body/eval_jaxpr/hqk,qhd->khd/dot_general | solution.py:132
  582.4 7.9 %fusion.125 = f32[1536,3,64]{0,2,1:T(8,128)} fusion(f32[1536,3,64]{0,2,1:T(8,128)} %scatter-add.16, bf16[512,3,64]{0,2,1:T(8,128)(2,1)S(1)} %bitcast.166, f32[3,512]{1,0:T(4,128)S(1)} %copy-done.63, pred[512,1024]{1,0:T(8,128)(4,1)S(1)} %copy-done.24, f32[3,512,1024]{2,1,0:T(8,128)} %copy-done.7), kind=kOutput, calls=%fused_computation.125 | convolution fusion | flops 212533248 | bytes 8591360 | tf_op jit(solution)/shard_map/while/body/eval_jaxpr/hqk,qhd->khd/dot_general | solution.py:140
  590.3 5.5 all-to-all-start.4
  598.2 8.8 %fusion.73 = bf16[1536,3,64]{0,2,1:T(8,128)(2,1)S(1)} fusion(f32[1536,3,64]{0,2,1:T(8,128)} %fusion.125, bf16[512,3,64]{0,2,1:T(8,128)(2,1)S(1)} %bitcast.160, f32[3,512]{1,0:T(4,128)S(1)} %copy-done.62, f32[3,512,1536]{2,1,0:T(8,128)} %copy-done.6, pred[512,1536]{1,0:T(8,128)(4,1)S(1)} %copy-done.17), kind=kOutput, calls=%fused_computation.93 | convolution fusion | flops 319094784 | bytes 12195840 | tf_op jit(solution)/shard_map/while/body/eval_jaxpr/hqk,qhd->khd/dot_general | solution.py:140
  616.4 7.8 %all-to-all-done.4 = bf16[8,96,768]{2,1,0:T(8,128)(2,1)} async-done(((bf16[8,96,768]{2,1,0:T(8,128)(2,1)}), bf16[8,96,768]{2,1,0:T(8,128)(2,1)}, u32[]{:S(2)}, u32[]{:S(2)}) %all-to-all-start.4) | async-done | bytes 1179680 | tf_op jit(solution)/shard_map/all_to_all | solution.py:18
  685.7 19.5 %all-reduce.11.cloned.1.call-done = (bf16[1536,768]{1,0:T(8,128)(2,1)}, bf16[1536,768]{1,0:T(8,128)(2,1)}) async-done(((bf16[1536,768]{1,0:T(8,128)(2,1)}, bf16[1536,768]{1,0:T(8,128)(2,1)}), (bf16[1536,768]{1,0:T(8,128)(2,1)}, bf16[1536,768]{1,0:T(8,128)(2,1)})) %all-reduce.11.cloned.1.call-update) | async-done | bytes 4718608 | tf_op jit(solution)/shard_map/psum | solution.py:206
  711.7 5.5 all-to-all-start.7
  717.4 5.2 multiply_convert_fusion.4
  726.3 6.0 all-to-all-start.6
  732.9 5.9 all-to-all-done.6
  (267 shorter events, 167.5 us)
Async XLA Ops:
  8.0 77.0 %copy-start.1 = (bf16[1536,768]{1,0:T(8,128)(2,1)S(1)}, bf16[1536,768]{1,0:T(8,128)(2,1)}, u32[]{:S(2)}) copy-start(bf16[1536,768]{1,0:T(8,128)(2,1)} %param.27) | copy-start | bytes 7077892
  8.0 45.9 %copy-start.50 = (bf16[96,192]{1,0:T(8,128)(2,1)S(1)}, bf16[96,192]{1,0:T(8,128)(2,1)}, u32[]{:S(2)}) copy-start(bf16[96,192]{1,0:T(8,128)(2,1)} %param.30) | copy-start | bytes 110596
  8.0 304.2 %all-reduce.7.cloned.1.call-start = ((), (), s32[]{:S(2)}) async-start(), calls=%async_computation.8 | async-start | bytes 9437184 | tf_op jit(solution)/shard_map/psum | solution.py:199
  32.3 53.9 %copy-start.46 = (f32[768]{0:T(1024)}, f32[768]{0:T(1024)S(1)}, u32[]{:S(2)}) copy-start(f32[768]{0:T(1024)S(1)} %get-tuple-element.217) | copy-start | bytes 9220
  51.4 35.7 %copy-start.37 = (f32[1536]{0:T(1024)}, f32[1536]{0:T(1024)S(1)}, u32[]{:S(2)}) copy-start(f32[1536]{0:T(1024)S(1)} %broadcast_multiply_fusion.5) | copy-start | bytes 18436
  53.9 31.0 %copy-start.44 = (f32[1536]{0:T(1024)}, f32[1536]{0:T(1024)S(1)}, u32[]{:S(2)}) copy-start(f32[1536]{0:T(1024)S(1)} %add_rsqrt_fusion.1) | copy-start | bytes 18436
  86.2 36.1 %copy-start.3 = (bf16[1536,768]{1,0:T(8,128)(2,1)}, bf16[1536,768]{1,0:T(8,128)(2,1)S(1)}, u32[]{:S(2)}) copy-start(bf16[1536,768]{1,0:T(8,128)(2,1)S(1)} %fusion.17) | copy-start | bytes 7077892
  87.1 116.7 %copy-start.21 = (bf16[1536,192]{0,1:T(8,128)(2,1)}, bf16[1536,192]{0,1:T(8,128)(2,1)S(1)}, u32[]{:S(2)}) copy-start(bf16[1536,192]{0,1:T(8,128)(2,1)S(1)} %convolution_convert_fusion.2) | copy-start | bytes 1769476
  125.1 66.2 %copy-start.43 = (bf16[512,192]{0,1:T(8,128)(2,1)S(1)}, bf16[512,192]{0,1:T(8,128)(2,1)}, u32[]{:S(2)}) copy-start(bf16[512,192]{0,1:T(8,128)(2,1)} %slice.337) | copy-start | bytes 589828
  156.4 60.1 %copy-start.14 = (bf16[192,768]{0,1:T(8,128)(2,1)}, bf16[192,768]{0,1:T(8,128)(2,1)S(1)}, u32[]{:S(2)}) copy-start(bf16[192,768]{0,1:T(8,128)(2,1)S(1)} %all_gather.29) | copy-start | bytes 884740
  191.2 18.3 %copy-start.16 = (pred[512,1536]{1,0:T(8,128)(4,1)}, pred[512,1536]{1,0:T(8,128)(4,1)S(1)}, u32[]{:S(2)}) copy-start(pred[512,1536]{1,0:T(8,128)(4,1)S(1)} %fusion.50) | copy-start | bytes 2359300
  219.5 100.0 %all-gather.5.cloned.1.call-start = ((), (), s32[]{:S(2)}) async-start(), calls=%async_computation.9 | async-start | bytes 1327104 | tf_op jit(solution)/shard_map/all_gather | solution.py:166
  220.1 105.6 %all-gather.7.cloned.1.call-start = ((), (), s32[]{:S(2)}) async-start(), calls=%async_computation.10 | async-start | bytes 1327104 | tf_op jit(solution)/shard_map/all_gather | solution.py:167
  220.7 212.0 %all-reduce.9.cloned.1.call-start = ((), (), s32[]{:S(2)}) async-start(), calls=%async_computation.11 | async-start | bytes 9437184 | tf_op jit(solution)/shard_map/psum | solution.py:214
  347.9 242.4 %all-to-all-start.5 = ((bf16[8,768,96]{1,2,0:T(8,128)(2,1)}), bf16[8,768,96]{1,2,0:T(8,128)(2,1)}, u32[]{:S(2)}, u32[]{:S(2)}) async-start(bf16[8,768,96]{1,2,0:T(8,128)(2,1)} %bitcast.158), calls=%async_computation.5 | async-start | bytes 2359296 | tf_op jit(solution)/shard_map/all_to_all | solution.py:18
  470.0 22.3 %copy-start.36 = (f32[512,3,64]{0,2,1:T(8,128)S(1)}, f32[512,3,64]{0,2,1:T(8,128)}, u32[]{:S(2)}) copy-start(f32[512,3,64]{0,2,1:T(8,128)} %fusion.128) | copy-start | bytes 1179652
  503.2 26.8 %copy-start.63 = (f32[3,512]{1,0:T(4,128)S(1)}, f32[3,512]{1,0:T(4,128)}, u32[]{:S(2)}) copy-start(f32[3,512]{1,0:T(4,128)} %log_add_fusion.1) | copy-start | bytes 18436
  530.0 20.4 %copy-start.40 = (bf16[512,192]{0,1:T(8,128)(2,1)S(1)}, bf16[512,192]{0,1:T(8,128)(2,1)}, u32[]{:S(2)}) copy-start(bf16[512,192]{0,1:T(8,128)(2,1)} %copy-done.39) | copy-start | bytes 589828
  550.5 27.8 %copy-start.13 = (bf16[768,192]{1,0:T(8,128)(2,1)S(1)}, bf16[768,192]{1,0:T(8,128)(2,1)}, u32[]{:S(2)}) copy-start(bf16[768,192]{1,0:T(8,128)(2,1)} %copy-done.12) | copy-start | bytes 884740
  590.3 34.0 %all-to-all-start.4 = ((bf16[8,96,768]{2,1,0:T(8,128)(2,1)}), bf16[8,96,768]{2,1,0:T(8,128)(2,1)}, u32[]{:S(2)}, u32[]{:S(2)}) async-start(bf16[8,96,768]{2,1,0:T(8,128)(2,1)} %bitcast.157), calls=%async_computation.4 | async-start | bytes 2359296 | tf_op jit(solution)/shard_map/all_to_all | solution.py:18
  595.8 109.4 %all-reduce.11.cloned.1.call-start = ((), (), s32[]{:S(2)}) async-start(), calls=%async_computation.12 | async-start | bytes 9437184 | tf_op jit(solution)/shard_map/psum | solution.py:206
  624.3 15.5 %all-to-all-start.2 = ((bf16[8,96,192]{1,2,0:T(8,128)(2,1)}), bf16[8,96,192]{1,2,0:T(8,128)(2,1)S(1)}, u32[]{:S(2)}, u32[]{:S(2)}) async-start(bf16[8,96,192]{1,2,0:T(8,128)(2,1)} %copy.78), calls=%async_computation.2 | async-start | bytes 786432 | tf_op jit(solution)/shard_map/all_to_all | solution.py:18
  639.7 15.6 %all-to-all-start = ((bf16[8,96,192]{1,2,0:T(8,128)(2,1)}), bf16[8,96,192]{1,2,0:T(8,128)(2,1)}, u32[]{:S(2)}, u32[]{:S(2)}) async-start(bf16[8,96,192]{1,2,0:T(8,128)(2,1)} %copy.74), calls=%async_computation | async-start | bytes 786432 | tf_op jit(solution)/shard_map/all_to_all | solution.py:18
  655.3 14.8 %all-to-all-start.1 = ((bf16[8,96,192]{1,2,0:T(8,128)(2,1)}), bf16[8,96,192]{1,2,0:T(8,128)(2,1)}, u32[]{:S(2)}, u32[]{:S(2)}) async-start(bf16[8,96,192]{1,2,0:T(8,128)(2,1)} %copy.76), calls=%async_computation.1 | async-start | bytes 786432 | tf_op jit(solution)/shard_map/all_to_all | solution.py:18
  661.6 43.6 %copy-start.38 = (f32[1536]{0:T(1024)S(1)}, f32[1536]{0:T(1024)}, u32[]{:S(2)}) copy-start(f32[1536]{0:T(1024)} %copy-done.37) | copy-start | bytes 18436
  661.6 43.6 %copy-start.45 = (f32[1536]{0:T(1024)S(1)}, f32[1536]{0:T(1024)}, u32[]{:S(2)}) copy-start(f32[1536]{0:T(1024)} %copy-done.44) | copy-start | bytes 18436
  665.5 39.7 %copy-start.47 = (f32[768]{0:T(1024)S(1)}, f32[768]{0:T(1024)}, u32[]{:S(2)}) copy-start(f32[768]{0:T(1024)} %copy-done.46) | copy-start | bytes 9220
  670.1 14.8 %all-to-all-start.3 = ((bf16[8,192,96]{2,1,0:T(8,128)(2,1)}), bf16[8,192,96]{2,1,0:T(8,128)(2,1)S(1)}, u32[]{:S(2)}, u32[]{:S(2)}) async-start(bf16[8,192,96]{2,1,0:T(8,128)(2,1)} %bitcast.139), calls=%async_computation.3 | async-start | bytes 786432 | tf_op jit(solution)/shard_map/all_to_all | solution.py:18
  677.7 39.7 %copy-start.56 = (f32[1536]{0:T(1024)S(1)}, f32[1536]{0:T(1024)}, u32[]{:S(2)}) copy-start(f32[1536]{0:T(1024)} %fusion.154) | copy-start | bytes 18436
  705.2 17.4 %slice-start = ((s8[4718592]{0:T(1024)(128)(4,1)}), s8[524288]{0:T(1024)(128)(4,1)S(1)}, s32[]{:S(2)}) async-start(s8[4718592]{0:T(1024)(128)(4,1)} %bitcast.145), calls=%async_computation.13 | async-start | bytes 1048576
  711.7 14.6 %all-to-all-start.7 = ((bf16[8,2,96]{2,1,0:T(2,128)(2,1)}), bf16[8,2,96]{2,1,0:T(2,128)(2,1)S(1)}, u32[]{:S(2)}, u32[]{:S(2)}) async-start(bf16[8,2,96]{2,1,0:T(2,128)(2,1)} %copy.82), calls=%async_computation.7 | async-start | bytes 8192 | tf_op jit(solution)/shard_map/all_to_all | solution.py:18
  726.3 12.5 %all-to-all-start.6 = ((bf16[8,2,96]{2,1,0:T(2,128)(2,1)}), bf16[8,2,96]{2,1,0:T(2,128)(2,1)S(1)}, u32[]{:S(2)}, u32[]{:S(2)}) async-start(bf16[8,2,96]{2,1,0:T(2,128)(2,1)} %copy.81), calls=%async_computation.6 | async-start | bytes 8192 | tf_op jit(solution)/shard_map/all_to_all | solution.py:18
  (53 other events, 255.0 us)
Sparse Core Ops, SparseCore 0:
  219.7 92.5 all-reduce.6
  338.5 94.1 all-reduce.8
  610.3 94.8 all-reduce.10
Sparse Core Ops, SparseCore 1:
  222.2 39.9 all-gather.4
  264.2 40.0 all-gather.6
where the time goes:
time: 757 us; the launch traced here: 747 us
  matrix products  231 us (31%)
  waiting for transfers between devices  205 us (27%)
  blocking collectives  163 us (22%)
  other arithmetic  57.6 us (8%)
  starting transfers between devices  38.8 us (5%)
  local copies, waits for them, and re-layouts  34.2 us (5%)
  between operations  17.1 us (2%)
    psum x1, waiting for transfers between devices, per_device(): hidden = inputs + lax.psum(attn_partial, 'tensor')  90.3 us
    psum x1, waiting for transfers between devices, per_device(): grad_normed_two = lax.psum(mid_partial, 'tensor')  66.6 us
    dot_general x3, matrix products, attend_back(): jnp.einsum('hqk,qhd->khd', grad_raw, queries[begin_row:end_row], preferre...  57.9 us
    dot_general x3, matrix products, attend_back(): jnp.einsum('hqk,khd->qhd', grad_raw, key_rows[:end_row], preferred_elemen...  56.7 us
    all_to_all x8, starting transfers between devices, summed_on_arrival(): lax.all_to_all(cut_along(value, dim, length), axis, 0, 0, tiled=True)  38.4 us
    all_gather x1, blocking collectives, per_device(): lax.all_gather(w_out, 'batch', axis=1, tiled=True)  31.3 us
    all_gather x1, blocking collectives, per_device(): lax.all_gather(w_value, 'batch', axis=0, tiled=True)  31.2 us
    all_gather x1, blocking collectives, per_device(): lax.all_gather(w_query, 'batch', axis=0, tiled=True)  31.2 us
  transfers between devices with their start and end apart: 13, of which 9 were waited for; matrix products, arithmetic and copies ran while one was open for 34% of the time, Pallas kernels for 0%

commit v1 on v0

--- a/solution.py
+++ b/solution.py
@@ -196,7 +196,8 @@
     )
     mixed_low = mixed_heads.reshape(seq_rows, head_count * HD).astype(jnp.bfloat16)
     attn_partial = multiply(mixed_low, full_out)
-    hidden = inputs + lax.psum(attn_partial, "tensor")
+    render_the_values = lambda q_in: jnp.sum(lax.all_gather(q_in, "tensor"), 0)
+    hidden = inputs + render_the_values(attn_partial)
     normed_two, scaled_two, inverse_two = normalize_keep(hidden, gain_rows[1], shift_rows[1])
     normed_two_low = normed_two.astype(jnp.bfloat16)
     up_proj = multiply(normed_two_low, full_up)

time: 757 us -> 852 us (1.13)
  waiting for transfers between devices: 205 us -> 291 us
  other arithmetic: 57.6 us -> 68.3 us
    all_gather x0 -> x1, waiting for transfers between devices: none -> 116 us  [per_device(): render_the_values = lambda q_in: jnp.sum(lax.all_gather(q_in, 'tensor'), 0)]
    psum x1 -> x0, waiting for transfers between devices: 90.3 us -> none  [per_device(): hidden = inputs + lax.psum(attn_partial, 'tensor')]
    all_gather x1, waiting for transfers between devices: 0.01 us -> 35.9 us  [per_device(): lax.all_gather(w_down, 'batch', axis=1, tiled=True)]
    all_gather x1, waiting for transfers between devices: 0.01 us -> 25.7 us  [per_device(): lax.all_gather(w_up, 'batch', axis=0, tiled=True)]
    reduce_sum x0 -> x1, other arithmetic: none -> 10.4 us  [per_device(): render_the_values = lambda q_in: jnp.sum(lax.all_gather(q_in, 'tensor'), 0)]
  transfers between devices with their start and end apart: 13 -> 13, of which waited for: 9 -> 11; matrix products, arithmetic and copies ran while one was open for 34% -> 31% of each run, Pallas kernels for 0% -> 0%
where the time goes in v1:
time: 852 us; the launch traced here: 842 us
  waiting for transfers between devices  291 us (34%)
  matrix products  232 us (27%)
  blocking collectives  163 us (19%)
  other arithmetic  68.3 us (8%)
  starting transfers between devices  37.5 us (4%)
  local copies, waits for them, and re-layouts  34.2 us (4%)
  between operations  15.5 us (2%)
    all_gather x1, waiting for transfers between devices, per_device(): render_the_values = lambda q_in: jnp.sum(lax.all_gather(q_in, 'tensor'), 0)  116 us
    psum x1, waiting for transfers between devices, per_device(): grad_normed_two = lax.psum(mid_partial, 'tensor')  65.9 us
    dot_general x3, matrix products, attend_back(): jnp.einsum('hqk,qhd->khd', grad_raw, queries[begin_row:end_row], preferre...  58.2 us
    dot_general x3, matrix products, attend_back(): jnp.einsum('hqk,khd->qhd', grad_raw, key_rows[:end_row], preferred_elemen...  56.3 us
    all_to_all x8, starting transfers between devices, summed_on_arrival(): lax.all_to_all(cut_along(value, dim, length), axis, 0, 0, tiled=True)  37 us
    all_gather x1, waiting for transfers between devices, per_device(): lax.all_gather(w_down, 'batch', axis=1, tiled=True)  35.9 us
    all_gather x1, blocking collectives, per_device(): lax.all_gather(w_out, 'batch', axis=1, tiled=True)  31.3 us
    all_gather x1, blocking collectives, per_device(): lax.all_gather(w_value, 'batch', axis=0, tiled=True)  31.2 us
  transfers between devices with their start and end apart: 13, of which 11 were waited for; matrix products, arithmetic and copies ran while one was open for 31% of the time, Pallas kernels for 0%

profile of v1, /device:TPU:0, one launch (start us, length us, event | category | flops | bytes accessed | tf_op | source)
XLA Modules:
  0.0 842.2 jit_solution(17484292192065140468)
XLA Ops:
  8.4 22.3 %all-gather.1 = bf16[8,96,2]{1,2,0:T(2,128)(2,1)S(1)} all-gather(bf16[1,96,2]{1,2,0:T(2,128)(2,1)} %bitcast.191), channel_id=1, replica_groups=mesh['batch'=8,'tensor'=4] {'batch'}, dimensions={0}, use_global_device_ids=true | all-gather | bytes 3456 | tf_op jit(solution)/shard_map/all_gather | solution.py:168
  31.4 16.4 %all-gather.2 = bf16[8,96,2]{1,2,0:T(2,128)(2,1)S(1)} all-gather(bf16[1,96,2]{1,2,0:T(2,128)(2,1)} %bitcast.192), channel_id=1, replica_groups=mesh['batch'=8,'tensor'=4] {'batch'}, dimensions={0}, use_global_device_ids=true | all-gather | bytes 3456 | tf_op jit(solution)/shard_map/all_gather | solution.py:169
  53.1 31.0 %all_gather.34 = bf16[768,192]{1,0:T(8,128)(2,1)S(1)} all-gather(bf16[96,192]{1,0:T(8,128)(2,1)S(1)} %copy-done.50), channel_id=1, replica_groups=mesh['batch'=8,'tensor'=4] {'batch'}, dimensions={0}, use_global_device_ids=true | all-gather | bytes 331776 | tf_op jit(solution)/shard_map/all_gather | solution.py:163
  87.8 31.2 %all_gather.32 = bf16[768,192]{1,0:T(8,128)(2,1)S(1)} all-gather(bf16[96,192]{1,0:T(8,128)(2,1)S(1)} %copy-done.51), channel_id=1, replica_groups=mesh['batch'=8,'tensor'=4] {'batch'}, dimensions={0}, use_global_device_ids=true | all-gather | bytes 331776 | tf_op jit(solution)/shard_map/all_gather | solution.py:164
  124.2 31.3 %all_gather.35 = bf16[192,768]{0,1:T(8,128)(2,1)S(1)} all-gather(bf16[192,96]{0,1:T(8,128)(2,1)} %copy.70), channel_id=1, replica_groups=mesh['batch'=8,'tensor'=4] {'batch'}, dimensions={1}, use_global_device_ids=true | all-gather | bytes 331776 | tf_op jit(solution)/shard_map/all_gather | solution.py:165
  155.6 31.2 %all_gather.33 = bf16[768,192]{1,0:T(8,128)(2,1)S(1)} all-gather(bf16[96,192]{1,0:T(8,128)(2,1)} %param.29), channel_id=1, replica_groups=mesh['batch'=8,'tensor'=4] {'batch'}, dimensions={0}, use_global_device_ids=true | all-gather | bytes 331776 | tf_op jit(solution)/shard_map/all_gather | solution.py:162
  209.5 6.4 fusion.150
  222.0 115.8 %all-gather.11.cloned.1.call-done = f32[6144,768]{1,0:T(8,128)} async-done(((f32[1536,768]{1,0:T(8,128)}), f32[6144,768]{1,0:T(8,128)}) %all-gather.11.cloned.1.call-update) | async-done | bytes 18874384 | tf_op jit(solution)/shard_map/all_gather | solution.py:199
  337.7 10.4 %reduce_sum.254 = f32[1536,768]{1,0:T(8,128)} reduce(f32[4,1536,768]{2,1,0:T(8,128)} %bitcast.150, f32[]{:T(128)} %constant.250.clone.1), dimensions={0}, to_apply=%region_8.9 | reduce | flops 3538944 | bytes 23592964 | tf_op jit(solution)/shard_map/reduce_sum | solution.py:199
  355.3 25.7 %all-gather.7.cloned.1.call-done = bf16[768,768]{1,0:T(8,128)(2,1)} async-done(((bf16[96,768]{1,0:T(8,128)(2,1)}), bf16[768,768]{1,0:T(8,128)(2,1)}) %all-gather.7.cloned.1.call-update) | async-done | bytes 1179664 | tf_op jit(solution)/shard_map/all_gather | solution.py:166
  381.0 6.1 fusion.203
  387.1 35.9 %all-gather.9.cloned.1.call-done = bf16[768,768]{0,1:T(8,128)(2,1)} async-done(((bf16[768,96]{0,1:T(8,128)(2,1)}), bf16[768,768]{0,1:T(8,128)(2,1)}) %all-gather.9.cloned.1.call-update) | async-done | bytes 1179664 | tf_op jit(solution)/shard_map/all_gather | solution.py:167
  423.1 7.0 fusion.31
  438.5 7.6 fusion.107
  450.6 5.5 convolution_convert_fusion.5
  456.2 6.7 convolution_convert_fusion
  462.9 65.9 %all-reduce.6.cloned.1.call-done = f32[1536,768]{1,0:T(8,128)} async-done(((f32[1536,768]{1,0:T(8,128)}), f32[1536,768]{1,0:T(8,128)}) %all-reduce.6.cloned.1.call-update) | async-done | bytes 4718608 | tf_op jit(solution)/shard_map/psum | solution.py:215
  528.8 5.6 multiply_reduce_fusion.2
  546.7 9.8 %fusion.128 = f32[512,3,64]{0,2,1:T(8,128)} fusion(bf16[512,3,64]{0,2,1:T(8,128)(2,1)} %bitcast.180, f32[3,512,512]{1,2,0:T(8,128)} %fusion.205, f32[3,512,512]{1,2,0:T(8,128)} %copy-done.18, f32[3,512]{1,0:T(4,128)S(1)} %copy-done.61, pred[512,512]{0,1:T(8,128)(4,1)} %copy-done.28), kind=kOutput, calls=%fused_computation.130 | convolution fusion | flops 114821120 | bytes 7149568 | tf_op jit(solution)/shard_map/while/body/eval_jaxpr/hqk,qhd->khd/dot_general | solution.py:132
  566.4 20.1 %fusion.145 = bf16[3,64,512]{2,1,0:T(8,128)(2,1)} fusion(bf16[1024,3,64]{0,2,1:T(8,128)(2,1)} %bitcast.173, f32[3,512,1024]{2,1,0:T(8,128)} %fusion.206, f32[3,512,1024]{2,1,0:T(8,128)} %copy-done.7, f32[3,512]{1,0:T(4,128)} %log_add_fusion.1, pred[512,1024]{1,0:T(8,128)(4,1)} %copy-done.23), kind=kOutput, calls=%fused_computation.139 | convolution fusion | flops 229739008 | bytes 13703168 | tf_op jit(solution)/shard_map/while/body/eval_jaxpr/hqk,khd->qhd/dot_general | solution.py:127
  589.8 9.8 %fusion.141 = bf16[3,64,512]{2,1,0:T(8,128)(2,1)} fusion(bf16[512,3,64]{0,2,1:T(8,128)(2,1)} %bitcast.181, f32[3,512,512]{1,2,0:T(8,128)} %fusion.205, f32[3,512,512]{1,2,0:T(8,128)} %copy-done.18, f32[3,512]{1,0:T(4,128)S(1)} %copy-done.61, pred[512,512]{0,1:T(8,128)(4,1)} %copy-done.28), kind=kOutput, calls=%fused_computation.137 | convolution fusion | flops 114919424 | bytes 6952960 | tf_op jit(solution)/shard_map/while/body/eval_jaxpr/hqk,khd->qhd/dot_general | solution.py:127
  599.6 26.4 %fusion.138 = bf16[3,64,512]{2,1,0:T(8,128)(2,1)} fusion(bf16[1536,3,64]{0,2,1:T(8,128)(2,1)S(1)} %bitcast.156, f32[3,512,1536]{2,1,0:T(8,128)} %fusion.207, f32[3,512,1536]{2,1,0:T(8,128)} %copy-done.6, f32[3,512]{1,0:T(4,128)S(1)} %copy-done.62, pred[512,1536]{1,0:T(8,128)(4,1)} %copy-done.16), kind=kOutput, calls=%fused_computation.136 | convolution fusion | flops 344558592 | bytes 20453376 | tf_op jit(solution)/shard_map/while/body/eval_jaxpr/hqk,khd->qhd/dot_general | solution.py:127
  626.0 20.5 %fusion.119 = f32[1536,3,64]{0,2,1:T(8,128)} fusion(f32[1536,3,64]{0,2,1:T(8,128)} %scatter-add.14, bf16[512,3,64]{0,2,1:T(8,128)(2,1)} %bitcast.178, f32[3,512,1024]{2,1,0:T(8,128)} %fusion.206, f32[3,512,1024]{2,1,0:T(8,128)} %copy-done.7, f32[3,512]{1,0:T(4,128)S(1)} %copy-done.63, pred[512,1024]{1,0:T(8,128)(4,1)} %copy-done.23), kind=kOutput, calls=%fused_computation.123 | convolution fusion | flops 229837312 | bytes 28000256 | tf_op jit(solution)/shard_map/while/body/eval_jaxpr/hqk,qhd->khd/dot_general | solution.py:132
  646.5 27.9 %fusion.76 = bf16[1536,3,64]{0,2,1:T(8,128)(2,1)} fusion(f32[1536,3,64]{0,2,1:T(8,128)} %fusion.119, bf16[512,3,64]{0,2,1:T(8,128)(2,1)S(1)} %bitcast.176, f32[3,512,1536]{2,1,0:T(8,128)} %fusion.207, f32[3,512,1536]{2,1,0:T(8,128)} %copy-done.6, f32[3,512]{1,0:T(4,128)S(1)} %copy-done.62, pred[512,1536]{1,0:T(8,128)(4,1)} %copy-done.16), kind=kOutput, calls=%fused_computation.94 | convolution fusion | flops 345050112 | bytes 21633024 | tf_op jit(solution)/shard_map/while/body/eval_jaxpr/hqk,qhd->khd/dot_general | solution.py:132
  678.5 7.9 fusion.125
  686.4 5.5 all-to-all-start.4
  694.3 8.8 %fusion.73 = bf16[1536,3,64]{0,2,1:T(8,128)(2,1)S(1)} fusion(f32[1536,3,64]{0,2,1:T(8,128)} %fusion.125, bf16[512,3,64]{0,2,1:T(8,128)(2,1)S(1)} %bitcast.162, f32[3,512]{1,0:T(4,128)S(1)} %copy-done.62, f32[3,512,1536]{2,1,0:T(8,128)} %copy-done.6, pred[512,1536]{1,0:T(8,128)(4,1)S(1)} %copy-done.17), kind=kOutput, calls=%fused_computation.93 | convolution fusion | flops 319094784 | bytes 12195840 | tf_op jit(solution)/shard_map/while/body/eval_jaxpr/hqk,qhd->khd/dot_general | solution.py:140
  712.5 7.9 all-to-all-done.4
  781.8 19.4 %all-reduce.8.cloned.1.call-done = (bf16[1536,768]{1,0:T(8,128)(2,1)}, bf16[1536,768]{1,0:T(8,128)(2,1)}) async-done(((bf16[1536,768]{1,0:T(8,128)(2,1)}, bf16[1536,768]{1,0:T(8,128)(2,1)}), (bf16[1536,768]{1,0:T(8,128)(2,1)}, bf16[1536,768]{1,0:T(8,128)(2,1)})) %all-reduce.8.cloned.1.call-update) | async-done | bytes 4718608 | tf_op jit(solution)/shard_map/psum | solution.py:207
  807.8 5.5 all-to-all-start.7
  822.4 6.0 all-to-all-start.6
  829.0 5.9 all-to-all-done.6
  (268 shorter events, 183.1 us)
Async XLA Ops:
  7.2 77.0 %copy-start.1 = (bf16[1536,768]{1,0:T(8,128)(2,1)S(1)}, bf16[1536,768]{1,0:T(8,128)(2,1)}, u32[]{:S(2)}) copy-start(bf16[1536,768]{1,0:T(8,128)(2,1)} %param.27) | copy-start | bytes 7077892
  7.2 45.9 %copy-start.50 = (bf16[96,192]{1,0:T(8,128)(2,1)S(1)}, bf16[96,192]{1,0:T(8,128)(2,1)}, u32[]{:S(2)}) copy-start(bf16[96,192]{1,0:T(8,128)(2,1)} %param.30) | copy-start | bytes 110596
  7.2 330.5 %all-gather.11.cloned.1.call-start = ((), (), s32[]{:S(2)}) async-start(), calls=%async_computation.11 | async-start | bytes 23592960 | tf_op jit(solution)/shard_map/all_gather | solution.py:199
  31.4 53.9 %copy-start.46 = (f32[768]{0:T(1024)}, f32[768]{0:T(1024)S(1)}, u32[]{:S(2)}) copy-start(f32[768]{0:T(1024)S(1)} %get-tuple-element.217) | copy-start | bytes 9220
  50.6 35.7 %copy-start.37 = (f32[1536]{0:T(1024)}, f32[1536]{0:T(1024)S(1)}, u32[]{:S(2)}) copy-start(f32[1536]{0:T(1024)S(1)} %broadcast_multiply_fusion.5) | copy-start | bytes 18436
  53.1 31.0 %copy-start.44 = (f32[1536]{0:T(1024)}, f32[1536]{0:T(1024)S(1)}, u32[]{:S(2)}) copy-start(f32[1536]{0:T(1024)S(1)} %add_rsqrt_fusion.1) | copy-start | bytes 18436
  85.3 36.1 %copy-start.3 = (bf16[1536,768]{1,0:T(8,128)(2,1)}, bf16[1536,768]{1,0:T(8,128)(2,1)S(1)}, u32[]{:S(2)}) copy-start(bf16[1536,768]{1,0:T(8,128)(2,1)S(1)} %fusion.17) | copy-start | bytes 7077892
  86.3 117.0 %copy-start.21 = (bf16[1536,192]{0,1:T(8,128)(2,1)}, bf16[1536,192]{0,1:T(8,128)(2,1)S(1)}, u32[]{:S(2)}) copy-start(bf16[1536,192]{0,1:T(8,128)(2,1)S(1)} %convolution_convert_fusion.2) | copy-start | bytes 1769476
  124.2 66.2 %copy-start.43 = (bf16[512,192]{0,1:T(8,128)(2,1)S(1)}, bf16[512,192]{0,1:T(8,128)(2,1)}, u32[]{:S(2)}) copy-start(bf16[512,192]{0,1:T(8,128)(2,1)} %slice.337) | copy-start | bytes 589828
  155.5 60.5 %copy-start.14 = (bf16[192,768]{0,1:T(8,128)(2,1)}, bf16[192,768]{0,1:T(8,128)(2,1)S(1)}, u32[]{:S(2)}) copy-start(bf16[192,768]{0,1:T(8,128)(2,1)S(1)} %all_gather.35) | copy-start | bytes 884740
  190.4 18.6 %copy-start.16 = (pred[512,1536]{1,0:T(8,128)(4,1)}, pred[512,1536]{1,0:T(8,128)(4,1)S(1)}, u32[]{:S(2)}) copy-start(pred[512,1536]{1,0:T(8,128)(4,1)S(1)} %fusion.50) | copy-start | bytes 2359300
  219.1 162.0 %all-gather.7.cloned.1.call-start = ((), (), s32[]{:S(2)}) async-start(), calls=%async_computation.8 | async-start | bytes 1327104 | tf_op jit(solution)/shard_map/all_gather | solution.py:166
  219.8 203.3 %all-gather.9.cloned.1.call-start = ((), (), s32[]{:S(2)}) async-start(), calls=%async_computation.9 | async-start | bytes 1327104 | tf_op jit(solution)/shard_map/all_gather | solution.py:167
  220.6 308.2 %all-reduce.6.cloned.1.call-start = ((), (), s32[]{:S(2)}) async-start(), calls=%async_computation.10 | async-start | bytes 9437184 | tf_op jit(solution)/shard_map/psum | solution.py:215
  446.1 240.2 %all-to-all-start.5 = ((bf16[8,768,96]{1,2,0:T(8,128)(2,1)}), bf16[8,768,96]{1,2,0:T(8,128)(2,1)}, u32[]{:S(2)}, u32[]{:S(2)}) async-start(bf16[8,768,96]{1,2,0:T(8,128)(2,1)} %bitcast.160), calls=%async_computation.5 | async-start | bytes 2359296 | tf_op jit(solution)/shard_map/all_to_all | solution.py:18
  566.4 22.2 %copy-start.36 = (f32[512,3,64]{0,2,1:T(8,128)S(1)}, f32[512,3,64]{0,2,1:T(8,128)}, u32[]{:S(2)}) copy-start(f32[512,3,64]{0,2,1:T(8,128)} %fusion.128) | copy-start | bytes 1179652
  599.5 26.4 %copy-start.63 = (f32[3,512]{1,0:T(4,128)S(1)}, f32[3,512]{1,0:T(4,128)}, u32[]{:S(2)}) copy-start(f32[3,512]{1,0:T(4,128)} %log_add_fusion.1) | copy-start | bytes 18436
  626.0 20.5 %copy-start.40 = (bf16[512,192]{0,1:T(8,128)(2,1)S(1)}, bf16[512,192]{0,1:T(8,128)(2,1)}, u32[]{:S(2)}) copy-start(bf16[512,192]{0,1:T(8,128)(2,1)} %copy-done.39) | copy-start | bytes 589828
  646.5 27.9 %copy-start.13 = (bf16[768,192]{1,0:T(8,128)(2,1)S(1)}, bf16[768,192]{1,0:T(8,128)(2,1)}, u32[]{:S(2)}) copy-start(bf16[768,192]{1,0:T(8,128)(2,1)} %copy-done.12) | copy-start | bytes 884740
  686.4 34.0 %all-to-all-start.4 = ((bf16[8,96,768]{2,1,0:T(8,128)(2,1)}), bf16[8,96,768]{2,1,0:T(8,128)(2,1)}, u32[]{:S(2)}, u32[]{:S(2)}) async-start(bf16[8,96,768]{2,1,0:T(8,128)(2,1)} %bitcast.159), calls=%async_computation.4 | async-start | bytes 2359296 | tf_op jit(solution)/shard_map/all_to_all | solution.py:18
  691.9 109.3 %all-reduce.8.cloned.1.call-start = ((), (), s32[]{:S(2)}) async-start(), calls=%async_computation.12 | async-start | bytes 9437184 | tf_op jit(solution)/shard_map/psum | solution.py:207
  720.4 15.5 %all-to-all-start.2 = ((bf16[8,96,192]{1,2,0:T(8,128)(2,1)}), bf16[8,96,192]{1,2,0:T(8,128)(2,1)S(1)}, u32[]{:S(2)}, u32[]{:S(2)}) async-start(bf16[8,96,192]{1,2,0:T(8,128)(2,1)} %copy.78), calls=%async_computation.2 | async-start | bytes 786432 | tf_op jit(solution)/shard_map/all_to_all | solution.py:18
  735.9 15.6 %all-to-all-start = ((bf16[8,96,192]{1,2,0:T(8,128)(2,1)}), bf16[8,96,192]{1,2,0:T(8,128)(2,1)}, u32[]{:S(2)}, u32[]{:S(2)}) async-start(bf16[8,96,192]{1,2,0:T(8,128)(2,1)} %copy.74), calls=%async_computation | async-start | bytes 786432 | tf_op jit(solution)/shard_map/all_to_all | solution.py:18
  751.4 14.9 %all-to-all-start.1 = ((bf16[8,96,192]{1,2,0:T(8,128)(2,1)}), bf16[8,96,192]{1,2,0:T(8,128)(2,1)}, u32[]{:S(2)}, u32[]{:S(2)}) async-start(bf16[8,96,192]{1,2,0:T(8,128)(2,1)} %copy.76), calls=%async_computation.1 | async-start | bytes 786432 | tf_op jit(solution)/shard_map/all_to_all | solution.py:18
  757.7 43.5 %copy-start.38 = (f32[1536]{0:T(1024)S(1)}, f32[1536]{0:T(1024)}, u32[]{:S(2)}) copy-start(f32[1536]{0:T(1024)} %copy-done.37) | copy-start | bytes 18436
  757.7 43.5 %copy-start.45 = (f32[1536]{0:T(1024)S(1)}, f32[1536]{0:T(1024)}, u32[]{:S(2)}) copy-start(f32[1536]{0:T(1024)} %copy-done.44) | copy-start | bytes 18436
  761.6 39.6 %copy-start.47 = (f32[768]{0:T(1024)S(1)}, f32[768]{0:T(1024)}, u32[]{:S(2)}) copy-start(f32[768]{0:T(1024)} %copy-done.46) | copy-start | bytes 9220
  766.3 14.8 %all-to-all-start.3 = ((bf16[8,192,96]{2,1,0:T(8,128)(2,1)}), bf16[8,192,96]{2,1,0:T(8,128)(2,1)S(1)}, u32[]{:S(2)}, u32[]{:S(2)}) async-start(bf16[8,192,96]{2,1,0:T(8,128)(2,1)} %bitcast.140), calls=%async_computation.3 | async-start | bytes 786432 | tf_op jit(solution)/shard_map/all_to_all | solution.py:18
  773.8 39.6 %copy-start.56 = (f32[1536]{0:T(1024)S(1)}, f32[1536]{0:T(1024)}, u32[]{:S(2)}) copy-start(f32[1536]{0:T(1024)} %fusion.154) | copy-start | bytes 18436
  801.2 17.4 %slice-start = ((s8[4718592]{0:T(1024)(128)(4,1)}), s8[524288]{0:T(1024)(128)(4,1)S(1)}, s32[]{:S(2)}) async-start(s8[4718592]{0:T(1024)(128)(4,1)} %bitcast.146), calls=%async_computation.13 | async-start | bytes 1048576
  807.8 14.6 %all-to-all-start.7 = ((bf16[8,2,96]{2,1,0:T(2,128)(2,1)}), bf16[8,2,96]{2,1,0:T(2,128)(2,1)S(1)}, u32[]{:S(2)}, u32[]{:S(2)}) async-start(bf16[8,2,96]{2,1,0:T(2,128)(2,1)} %copy.82), calls=%async_computation.7 | async-start | bytes 8192 | tf_op jit(solution)/shard_map/all_to_all | solution.py:18
  822.4 12.5 %all-to-all-start.6 = ((bf16[8,2,96]{2,1,0:T(2,128)(2,1)}), bf16[8,2,96]{2,1,0:T(2,128)(2,1)S(1)}, u32[]{:S(2)}, u32[]{:S(2)}) async-start(bf16[8,2,96]{2,1,0:T(2,128)(2,1)} %copy.81), calls=%async_computation.6 | async-start | bytes 8192 | tf_op jit(solution)/shard_map/all_to_all | solution.py:18
  (53 other events, 256.7 us)
Sparse Core Ops, SparseCore 0:
  219.2 118.5 all-gather.10
  339.9 41.0 all-gather.6
  383.2 39.8 all-gather.8
  436.0 92.7 all-reduce.5
  706.4 94.8 all-reduce.7
